TPU v7x, 32 devices: a whole 2x2x4 slice. The times are simulated.
32 devices in a mesh: scan: 8 (over z, y), beam: 4 (over x, core).
Axes of the slice: x: 2, y: 2, z: 4, core: 2. Of those that a mesh axis runs over, the one named last changes fastest.
Arguments:
- smatrix: bfloat16 [2, 1024, 512, 128], P(None, 'beam', 'scan'), may hold values from -6 to 6
- beam_freq: int32 [2, 1024], P(None, 'beam'), may hold values from -32 to 31
- beam_amp: float32 [2, 1024], P(None, 'beam'), may hold values from -0.1875 to 0.1875
- row_offset: int32 [512], P('scan'), may hold values from 0 to 63
- col_offset: int32 [512], P('scan'), may hold values from 0 to 127
- counts: int32 [8], P('scan'), may hold values from 16 to 64, as said below
- amplitude: float32 [512, 128, 128], P('scan'), may hold values from 0.25 to 2
Outputs:
- grad_smatrix: bfloat16 [2, 1024, 512, 128], P(None, 'beam', 'scan')
Inputs may be any that keep to these rules, and one draw needn't show every extreme that they name: `counts`: slots of a tile at or past its count are unused; some tile holds exactly 64 live positions.
All inputs are finite; a program needn't handle non-finite values.
Results may differ from a plain program's by a relative error of at most 0.0063.
Values may be sent and summed in bfloat16 or wider, within the bound.
A program may use at most 192 MiB of HBM per device.

v0:
```python
import functools

import jax
import jax.numpy as jnp
import numpy as np
from jax import lax
from jax.experimental import pallas as pl
from jax.experimental.pallas import tpu as pltpu
from jax.sharding import PartitionSpec as P

TWO_PI = 6.283185307179586
ETA = 0.1
F32 = jnp.float32
BF16 = jnp.bfloat16
MESH = pl.DeviceIdType.MESH


def split_two(value):
    high = value.astype(BF16)
    return high, (value - high.astype(F32)).astype(BF16)


def three_products(left_high, left_low, right_high, right_low):
    total = jnp.dot(left_low, right_high, preferred_element_type=F32)
    total += jnp.dot(left_high, right_low, preferred_element_type=F32)
    return total + jnp.dot(left_high, right_high, preferred_element_type=F32)


def wave_kernel(shares, scan_size, spots_ref, freq_ref, amp_ref, live_ref, tables_ref, strip_ref,
                amplitude_ref, parts_ref, matrix_ref, offset_ref,
                spots, strips, wide, kept, core_out, core_in, link_out, link_in, zed_out, zed_in,
                scan_out, scan_in, near, far, measured, waves, backs, own_far,
                load_sem, amp_sem, spot_send, spot_recv, pair_send, pair_recv, link_send, link_recv,
                zed_send, zed_recv, scan_send, scan_recv,
                hop_send, hop_recv, step_send, step_recv, join_send, join_recv):
    chunks, pairs, _, block_rows, group, window = kept.shape
    _, _, groups, strip_rows, depth, _ = parts_ref.shape
    beams = strip_ref.shape[1]
    share = depth // 2
    share_rows = group // 2
    field_rows = strip_rows * scan_size
    me = lax.axis_index("beam")
    tile = lax.axis_index("scan")
    core_id = me + 1 - 2 * lax.rem(me, 2)
    core_mate = {"beam": core_id}
    link_mate = {"beam": lax.rem(me + pairs, shares)}
    share_ids = [me, lax.rem(me + pairs, shares), core_id, lax.rem(core_id + pairs, shares)]
    before = [{"scan": lax.rem(tile + scan_size - d, scan_size)} for d in (1, 2)]
    after = [{"scan": lax.rem(tile + d, scan_size)} for d in (1, 2)]

    def load(chunk):
        return pltpu.make_async_copy(
            strip_ref.at[:, :, pl.ds(chunk * block_rows, block_rows), :],
            strips.at[chunk % 2],
            load_sem.at[chunk % 2],
        )

    def remote(source, target, sends, recvs, device):
        return pltpu.make_async_remote_copy(
            source, target, sends, recvs, device_id=device, device_id_type=MESH
        )

    def spot_copy(d):
        return remote(spots_ref, spots.at[d - 1], spot_send.at[d - 1], spot_recv.at[d - 1], after[d - 1])

    load(0).start()
    load(1).start()
    load_amplitude = pltpu.make_async_copy(
        amplitude_ref.at[pl.ds(me * share_rows, share_rows)], measured, amp_sem
    )
    load_amplitude.start()
    barrier = pltpu.get_barrier_semaphore()
    peers = [core_mate, link_mate] + before + after
    for peer in peers:
        pl.semaphore_signal(barrier, inc=1, device_id=peer, device_id_type=MESH)
    pl.semaphore_wait(barrier, len(peers))
    spot_copy(1).start()
    spot_copy(2).start()

    def coefficients(d):
        source = spots_ref if d == 0 else spots.at[d - 1]
        tile_id = lax.rem(tile + scan_size - d, scan_size)
        for s in range(shares):
            here = pl.ds(share_ids[s] * share_rows, share_rows)
            rows = source[0, here, :]
            cols = source[1, here, :]
            base = (d * shares + s) * group
            if d != 1:
                at = s * group
                for g in range(groups):
                    own = rows[g * share : (g + 1) * share]
                    offset_ref[d // 2, at + g * depth : at + (g + 1) * depth, :] = jnp.concatenate(
                        [own, own], axis=0
                    )
            for lane in range(0, beams, window):
                lanes = slice(lane, lane + window)
                along_rows = (freq_ref[0:1, lanes] * (tile_id * strip_rows + rows)) & (field_rows - 1)
                along_cols = (freq_ref[1:2, lanes] * cols) & (window - 1)
                turns = along_rows.astype(F32) / field_rows + along_cols.astype(F32) / window
                angle = -TWO_PI * turns
                cos_part = jnp.cos(angle)
                sin_part = jnp.sin(angle)
                coef_re = amp_ref[0:1, lanes] * cos_part - amp_ref[1:2, lanes] * sin_part
                coef_im = amp_ref[0:1, lanes] * sin_part + amp_ref[1:2, lanes] * cos_part
                for g in range(groups):
                    re = coef_re[g * share : (g + 1) * share]
                    im = coef_im[g * share : (g + 1) * share]
                    spot = slice(base + g * depth, base + (g + 1) * depth)
                    matrix_ref[spot, lanes] = jnp.concatenate([re, im], axis=0).astype(BF16)
                    matrix_ref[spot, beams + lane : beams + lane + window] = jnp.concatenate(
                        [-im, re], axis=0
                    ).astype(BF16)

    coefficients(0)
    for d in (1, 2):
        spot_copy(d).wait()
        coefficients(d)

    def to_core(chunk):
        return remote(
            core_out.at[chunk], core_in.at[chunk], pair_send.at[chunk], pair_recv.at[chunk], core_mate
        )

    def to_link(g, chunk, late):
        if chunk >= chunks // 2:
            pieces = slice(0, 3)
        elif late:
            pieces = slice(0, 1)
        else:
            pieces = slice(1, 2)
        pieces = pl.ds(pieces.start, pieces.stop - pieces.start)
        return remote(
            link_out.at[g, chunk, pieces], link_in.at[g, chunk, pieces],
            link_send.at[g, chunk, late], link_recv.at[g, chunk, late], link_mate,
        )

    def to_zed(g, chunk):
        return remote(
            zed_out.at[g, chunk], zed_in.at[g, chunk],
            zed_send.at[g, chunk], zed_recv.at[g, chunk], before[1],
        )

    def to_scan(g, chunk, which):
        return remote(
            scan_out.at[g, chunk, which], scan_in.at[g, chunk, which],
            scan_send.at[g, chunk, which], scan_recv.at[g, chunk, which], before[which],
        )

    def compute(chunk):
        load(chunk).wait()
        wide[...] = strips[chunk % 2].astype(F32).reshape(2 * beams * block_rows, window)
        if chunk + 2 < chunks:
            load(chunk + 2).start()

        def pair_of_rows(step, carry):
            row = step * 2
            rhs = jnp.concatenate(
                [wide[pl.ds(row + k, 2 * beams, stride=block_rows), :] for k in range(2)], axis=1
            ).astype(BF16)
            sums = jnp.dot(matrix_ref[...], rhs, preferred_element_type=F32)
            for k in range(2):
                here = chunk * block_rows + row + k
                for d in range(3):
                    for s in range(shares):
                        at = (d * shares + s) * group
                        piece = sums[at : at + group, k * window : (k + 1) * window]
                        if d == 0:
                            piece = jnp.where(here >= offset_ref[0, s * group : (s + 1) * group], piece, 0.0)
                        if d == 2:
                            piece = jnp.where(here < offset_ref[1, s * group : (s + 1) * group], piece, 0.0)
                        if s < pairs:
                            kept[chunk, s, d, row + k] = piece
                        else:
                            core_out[chunk, s - pairs, d, row + k] = piece.astype(BF16)
            return carry

        lax.fori_loop(0, block_rows // 2, pair_of_rows, 0)
        to_core(chunk).start()

    def held(g, chunk, s, d):
        part = slice(g * depth, (g + 1) * depth)
        return kept[chunk, s, d, :, part, :] + core_in[chunk, s, d, :, part, :].astype(F32)

    def after_core(g, chunk):
        if g == 0:
            to_core(chunk).wait_recv()
        link_out[g, chunk, 1] = held(g, chunk, 1, 1).astype(BF16)
        if chunk < chunks // 2:
            for s in range(2):
                zed_out[g, chunk, s] = held(g, chunk, s, 2).astype(BF16)
            to_zed(g, chunk).start()
        else:
            for d in (0, 2):
                link_out[g, chunk, d] = held(g, chunk, 1, d).astype(BF16)
        to_link(g, chunk, 0).start()

    def after_zed(g, chunk):
        to_zed(g, chunk).wait_recv()
        link_out[g, chunk, 0] = (held(g, chunk, 1, 0) + zed_in[g, chunk, 1].astype(F32)).astype(BF16)
        to_link(g, chunk, 1).start()

    def rows_of(chunk):
        return slice(chunk * block_rows, (chunk + 1) * block_rows)

    def after_link(g, chunk):
        to_link(g, chunk, 0).wait_recv()
        for d in (1, 2) if chunk >= chunks // 2 else (1,):
            scan_out[g, chunk, d - 1] = (
                held(g, chunk, 0, d) + link_in[g, chunk, d].astype(F32)
            ).astype(BF16)
            to_scan(g, chunk, d - 1).start()
        if chunk >= chunks // 2:
            near[g, rows_of(chunk)] = held(g, chunk, 0, 0) + link_in[g, chunk, 0].astype(F32)

    def finish(g, chunk):
        if chunk < chunks // 2:
            to_link(g, chunk, 1).wait_recv()
            near[g, rows_of(chunk)] = (
                held(g, chunk, 0, 0)
                + zed_in[g, chunk, 0].astype(F32)
                + link_in[g, chunk, 0].astype(F32)
            )
        to_scan(g, chunk, 0).wait_recv()
        far[g, rows_of(chunk)] = scan_in[g, chunk, 0].astype(F32)
        if chunk >= chunks // 2:
            to_scan(g, chunk, 1).wait_recv()
            near[g, rows_of(chunk)] += scan_in[g, chunk, 1].astype(F32)

    half_rows = strip_rows // 2
    halves = [pl.ds(h * half_rows, half_rows) for h in range(2)]
    hop_at = {(0, 0): 0, (0, 1): 1, (1, 0): 2, (1, 1): 3, (2, 0): 4}
    step_at = {(1, 0, 0): 0, (1, 0, 1): 1, (2, 0, 0): 2, (2, 0, 1): 3, (2, 1, 1): 4}

    def over_link(d, g, h):
        at = hop_at[d, h]
        return remote(
            parts_ref.at[d, 0, g, halves[h]], parts_ref.at[d, 1, g, halves[h]],
            hop_send.at[g, at], hop_recv.at[g, at], link_mate,
        )

    def over_core(d, s, g, h):
        at = d * 2 + s
        return remote(
            parts_ref.at[d, s, g, halves[h]], parts_ref.at[d, s + 2, g, halves[h]],
            join_send.at[g, at, h], join_recv.at[g, at, h], core_mate,
        )

    def over_scan(d, s, g, h):
        at = step_at[d, s, h]
        source = own_far.at[g] if d == 1 else parts_ref.at[0, s, g]
        return remote(
            source.at[halves[h]], parts_ref.at[d, s, g, halves[h]],
            step_send.at[g, at], step_recv.at[g, at], after[d - 1],
        )

    def by_columns(high, low, table):
        return three_products(high, low, tables_ref[table], tables_ref[table + 1])

    def transform(g):
        rows = strip_rows * share
        for half in range(2):
            block = (near if half == 0 else far)[g]
            tall = jnp.concatenate(
                [block[:, :share].reshape(rows, window), block[:, share:].reshape(rows, window)], axis=1
            )
            high, low = split_two(tall)
            done = by_columns(high, low, 0)
            for c in range(2):
                waves[c, half * rows : (half + 1) * rows, :] = done[:, c * window : (c + 1) * window]

        for p in range(0, share, 2):
            columns = []
            for k in range(2):
                columns.append(
                    jnp.concatenate(
                        [waves[c, pl.ds(p + k, window, stride=share), :] for c in range(2)], axis=0
                    )
                )
            high, low = split_two(jnp.concatenate(columns, axis=1))
            wave = three_products(tables_ref[4], tables_ref[5], high, low)
            wave_re, wave_im = wave[:window], wave[window:]
            at = g * share + p
            values = jnp.concatenate([measured[at], measured[at + 1]], axis=1)
            modulus = jnp.sqrt(wave_re * wave_re + wave_im * wave_im + ETA)
            keep_share = 1.0 - values / modulus
            high, low = split_two(jnp.concatenate([wave_re * keep_share, wave_im * keep_share], axis=0))
            back = three_products(tables_ref[6], tables_ref[7], high, low)
            for k in range(2):
                for c in range(2):
                    backs[c, pl.ds(p + k, window, stride=share), :] = back[
                        c * window : (c + 1) * window, k * window : (k + 1) * window
                    ]

        live = live_ref[g * share : (g + 1) * share][None]
        for half in (1, 0):
            tall = jnp.concatenate(
                [backs[c, half * rows : (half + 1) * rows, :] for c in range(2)], axis=1
            )
            high, low = split_two(tall)
            done = by_columns(high, low, 2)
            pieces = [
                done[:, c * window : (c + 1) * window].reshape(strip_rows, share, window) * live
                for c in range(2)
            ]
            value = jnp.concatenate(pieces, axis=1).astype(BF16)
            if half:
                own_far[g] = value
                for h in range(2):
                    over_scan(1, 0, g, h).start()
            else:
                parts_ref[0, 0, g] = value
                for h in (1, 0):
                    over_link(0, g, h).start()
                for h in range(2):
                    over_scan(2, 0, g, h).start()
                    over_core(0, 0, g, h).start()

    def got_scan(d, s, g, h, link):
        over_scan(d, s, g, h).wait_recv()
        if link:
            over_link(d, g, h).start()
        over_core(d, s, g, h).start()

    def got_link(d, g, h, scan):
        over_link(d, g, h).wait_recv()
        if scan:
            over_scan(2, 1, g, h).start()
        over_core(d, 1, g, h).start()

    def relay(g):
        got_scan(1, 0, g, 0, True)
        got_scan(1, 0, g, 1, True)
        got_link(0, g, 1, True)
        got_link(0, g, 0, False)
        got_scan(2, 0, g, 0, True)
        got_scan(2, 0, g, 1, False)
        got_link(1, g, 0, False)
        got_link(1, g, 1, False)
        got_scan(2, 1, g, 1, False)
        got_link(2, g, 0, False)

    early = range(chunks // 2)
    for chunk in range(chunks):
        compute(chunk)
        if chunk:
            after_core(0, chunk - 1)
    after_core(0, chunks - 1)
    for chunk in early:
        after_zed(0, chunk)
    for chunk in range(chunks):
        after_core(1, chunk)
    for chunk in range(chunks):
        after_link(0, chunk)
    for chunk in early:
        after_zed(1, chunk)
    for chunk in range(chunks):
        finish(0, chunk)
    load_amplitude.wait()
    transform(0)
    for chunk in range(chunks):
        after_link(1, chunk)
    for chunk in range(chunks):
        finish(1, chunk)
    transform(1)
    for g in range(groups):
        relay(g)

    for chunk in range(chunks):
        to_core(chunk).wait_send()
        for g in range(groups):
            to_link(g, chunk, 0).wait_send()
            to_scan(g, chunk, 0).wait_send()
            if chunk < chunks // 2:
                to_link(g, chunk, 1).wait_send()
                to_zed(g, chunk).wait_send()
            else:
                to_scan(g, chunk, 1).wait_send()
    for g in range(groups):
        for d in range(3):
            for s in range(2):
                for h in range(2):
                    over_core(d, s, g, h).wait()
        for d, h in hop_at:
            over_link(d, g, h).wait_send()
        for d, s, h in step_at:
            over_scan(d, s, g, h).wait_send()


def waves_to_gradients(spots, freq, amp, live, tables, strip, amplitude, shares, scan_size,
                       groups=2, block_rows=8):
    _, beams, strip_rows, window = strip.shape
    per_tile = spots.shape[1]
    share_rows = per_tile // shares
    group = 2 * share_rows
    depth = group // groups
    field_rows = strip_rows * scan_size
    chunks = strip_rows // block_rows
    pairs = shares // 2
    assert groups == 2 and shares == 4 and scan_size > 4 and chunks % 2 == 0
    assert field_rows & (field_rows - 1) == 0 and window & (window - 1) == 0
    tail = (block_rows, depth, window)
    vmem = pl.BlockSpec(memory_space=pltpu.VMEM)
    anywhere = pl.BlockSpec(memory_space=pl.ANY)
    dma = pltpu.SemaphoreType.DMA
    return pl.pallas_call(
        functools.partial(wave_kernel, shares, scan_size),
        out_shape=[
            jax.ShapeDtypeStruct((3, shares, groups, strip_rows, depth, window), BF16),
            jax.ShapeDtypeStruct((3 * shares * group, 2 * beams), BF16),
            jax.ShapeDtypeStruct((2, shares * group, window), jnp.int32),
        ],
        in_specs=[vmem] * 5 + [anywhere] * 2,
        out_specs=[vmem] * 3,
        scratch_shapes=[
            pltpu.VMEM((2, 2, per_tile, window), jnp.int32),
            pltpu.VMEM((2, 2, beams, block_rows, window), BF16),
            pltpu.VMEM((2 * beams * block_rows, window), F32),
            pltpu.VMEM((chunks, pairs, 3, block_rows, group, window), F32),
            pltpu.VMEM((chunks, pairs, 3, block_rows, group, window), BF16),
            pltpu.VMEM((chunks, pairs, 3, block_rows, group, window), BF16),
            pltpu.VMEM((groups, chunks, 3) + tail, BF16),
            pltpu.VMEM((groups, chunks, 3) + tail, BF16),
            pltpu.VMEM((groups, chunks // 2, 2) + tail, BF16),
            pltpu.VMEM((groups, chunks // 2, 2) + tail, BF16),
            pltpu.VMEM((groups, chunks, 2) + tail, BF16),
            pltpu.VMEM((groups, chunks, 2) + tail, BF16),
            pltpu.VMEM((groups, strip_rows, depth, window), F32),
            pltpu.VMEM((groups, strip_rows, depth, window), F32),
            pltpu.VMEM((share_rows, window, window), F32),
            pltpu.VMEM((2, window * share_rows // groups, window), F32),
            pltpu.VMEM((2, window * share_rows // groups, window), F32),
            pltpu.VMEM((groups, strip_rows, depth, window), BF16),
            dma((2,)),
            dma,
            dma((2,)),
            dma((2,)),
            dma((chunks,)),
            dma((chunks,)),
            dma((groups, chunks, 2)),
            dma((groups, chunks, 2)),
            dma((groups, chunks // 2)),
            dma((groups, chunks // 2)),
            dma((groups, chunks, 2)),
            dma((groups, chunks, 2)),
            dma((groups, 5)),
            dma((groups, 5)),
            dma((groups, 5)),
            dma((groups, 5)),
            dma((groups, 6, 2)),
            dma((groups, 6, 2)),
        ],
        compiler_params=pltpu.CompilerParams(
            collective_id=0, has_side_effects=True, vmem_limit_bytes=48 << 20
        ),
        cost_estimate=pl.CostEstimate(
            flops=12 * per_tile * beams * strip_rows * window,
            bytes_accessed=4 * beams * strip_rows * window,
            transcendentals=0,
        ),
    )(spots, freq, amp, live, tables, strip, amplitude)


def backward_kernel(block_rows, offset_ref, matrix_ref, parts_ref, out_ref, wide):
    depth = matrix_ref.shape[0]
    window = out_ref.shape[3]
    first = pl.program_id(0) * block_rows
    kinds, shares, groups = parts_ref.shape[:3]
    for row in range(0, block_rows, 2):
        sides = []
        for k in range(2):
            here = first + row + k
            strips = []
            for d in range(kinds):
                tall = jnp.concatenate(
                    [parts_ref[d, s, g, row + k] for s in range(shares) for g in range(groups)], axis=0
                )
                if d == 0:
                    tall = jnp.where(here >= offset_ref[0], tall.astype(F32), 0.0).astype(BF16)
                if d == 2:
                    tall = jnp.where(here < offset_ref[1], tall.astype(F32), 0.0).astype(BF16)
                strips.append(tall)
            sides.append(jnp.concatenate(strips, axis=0))
        sums = jnp.dot(
            matrix_ref[...], jnp.concatenate(sides, axis=1), preferred_element_type=F32
        )
        for k in range(2):
            wide[pl.ds(row + k, depth, stride=block_rows), :] = sums[:, k * window : (k + 1) * window]
    out_ref[...] = wide[...].reshape(out_ref.shape).astype(BF16)


def backward(matrix, offsets, parts, beams, block_rows=8):
    kinds, shares, groups, strip_rows, depth, window = parts.shape
    return pl.pallas_call(
        functools.partial(backward_kernel, block_rows),
        grid=(strip_rows // block_rows,),
        out_shape=jax.ShapeDtypeStruct((2, beams, strip_rows, window), BF16),
        in_specs=[
            pl.BlockSpec(offsets.shape, lambda i: (0, 0, 0)),
            pl.BlockSpec(matrix.shape, lambda i: (0, 0)),
            pl.BlockSpec(
                (kinds, shares, groups, block_rows, depth, window), lambda i: (0, 0, 0, i, 0, 0)
            ),
        ],
        out_specs=pl.BlockSpec((2, beams, block_rows, window), lambda i: (0, 0, i, 0)),
        scratch_shapes=[pltpu.VMEM((2 * beams * block_rows, window), F32)],
        compiler_params=pltpu.CompilerParams(vmem_limit_bytes=28 << 20),
        cost_estimate=pl.CostEstimate(
            flops=2 * matrix.size * strip_rows * window,
            bytes_accessed=4 * beams * strip_rows * window + 2 * parts.size,
            transcendentals=0,
        ),
    )(offsets, matrix, parts)


def transform_tables(window):
    counter = np.arange(window)
    turn_angle = (counter[:, None] * counter[None, :] % window) * (2.0 * np.pi / window)
    table_re = np.cos(turn_angle) / np.sqrt(window)
    table_im = -np.sin(turn_angle) / np.sqrt(window)
    stacked = []
    for left in (False, True):
        for sign in (1.0, -1.0):
            imag = sign * table_im
            if left:
                full = np.block([[table_re, -imag], [imag, table_re]])
            else:
                full = np.block([[table_re, imag], [-imag, table_re]])
            high = full.astype(BF16)
            stacked += [high, (full - high.astype(np.float64)).astype(BF16)]
    return jnp.asarray(np.stack(stacked))


def body(smatrix, beam_freq, beam_amp, row_offset, col_offset, counts, amplitude):
    beam_dev = smatrix.shape[1]
    window = smatrix.shape[3]
    per_tile = row_offset.shape[0]
    scan_size = lax.axis_size("scan")
    shares = lax.axis_size("beam")
    share_rows = per_tile // shares
    assert window == 2 * smatrix.shape[2]
    spots = jnp.broadcast_to(
        jnp.stack([row_offset, col_offset])[:, :, None], (2, per_tile, window)
    )
    first_row = lax.axis_index("beam") * share_rows
    live = (first_row + jnp.arange(share_rows, dtype=jnp.int32) < counts[0]).astype(F32)
    live = jnp.broadcast_to(live[:, None], (share_rows, window))
    parts, matrix, offsets = waves_to_gradients(
        spots, beam_freq, beam_amp, live, transform_tables(window), smatrix, amplitude, shares, scan_size
    )
    return backward(matrix.T, offsets, parts, beam_dev)


def solution(mesh):
    return jax.shard_map(
        body,
        mesh=mesh,
        in_specs=(
            P(None, "beam", "scan", None),
            P(None, "beam"),
            P(None, "beam"),
            P("scan"),
            P("scan"),
            P("scan"),
            P("scan", None, None),
        ),
        out_specs=P(None, "beam", "scan", None),
        check_vma=False,
    )
```

profile of v0, /device:TPU:5, one launch (start us, length us, event | category | flops | bytes accessed | tf_op | source)
XLA Modules:
  0.0 107.5 jit_solution(14467748822550599389)
XLA Ops:
  0.7 0.7 pad_add_fusion
  1.3 0.1 broadcast_in_dim.5.live_ref
  1.4 0.1 broadcast_in_dim.4.spots_ref
  1.5 0.0 copy-start.1
  1.5 2.2 %copy-done.1 = f32[64,128,128]{2,1,0:T(8,128)S(1)} copy-done((f32[64,128,128]{2,1,0:T(8,128)S(1)}, f32[64,128,128]{2,1,0:T(8,128)}, u32[]{:S(2)}) %copy-start.1) | copy-done | bytes 4194328
  3.7 0.0 copy-start.2
  3.7 1.2 %copy-done.2 = bf16[8,256,256]{2,1,0:T(8,128)(2,1)S(1)} copy-done((bf16[8,256,256]{2,1,0:T(8,128)(2,1)S(1)}, bf16[8,256,256]{2,1,0:T(8,128)(2,1)}, u32[]{:S(2)}) %copy-start.2) | copy-done | bytes 1048600
  4.9 0.0 copy-start.3
  4.9 0.7 copy-done.3
  5.6 0.0 copy-start.4
  5.6 0.7 copy-done.4
  6.3 89.7 %shard_map.82 = (bf16[3,4,2,64,16,128]{5,4,3,2,1,0:T(8,128)(2,1)}, bf16[384,512]{1,0:T(8,128)(2,1)S(1)}, s32[2,128,128]{2,1,0:T(8,128)S(1)}) custom-call(s32[2,64,128]{2,1,0:T(8,128)S(1)} %broadcast_in_dim.4.spots_ref, s32[2,256]{1,0:T(2,128)S(1)} %copy-done.3, f32[2,256]{1,0:T(2,128)S(1)} %copy-done.4, f32[16,128]{1,0:T(8,128)S(1)} %broadcast_in_dim.5.live_ref, ...), custom_call_target="tpu_custom_call" | custom-call | flops 1610612736 | bytes 8388608 | tf_op jit(solution)/shard_map/pallas_call | solution.py:405
  96.0 0.2 copy.9
  96.2 0.0 copy-start
  96.2 2.8 %copy-done = bf16[3,4,2,64,16,128]{5,4,3,2,1,0:T(8,128)(2,1)S(1)} copy-done((bf16[3,4,2,64,16,128]{5,4,3,2,1,0:T(8,128)(2,1)S(1)}, bf16[3,4,2,64,16,128]{5,4,3,2,1,0:T(8,128)(2,1)}, u32[]{:S(2)}) %copy-start) | copy-done | bytes 6291480
  99.0 8.5 %shard_map.83 = bf16[2,256,64,128]{3,2,1,0:T(8,128)(2,1)} custom-call(s32[2,128,128]{2,1,0:T(8,128)S(1)} %get-tuple-element.8.offset_ref, bf16[512,384]{1,0:T(8,128)(2,1)S(1)} %bitcast.5, bf16[3,4,2,64,16,128]{5,4,3,2,1,0:T(8,128)(2,1)S(1)} %copy-done), custom_call_target="tpu_custom_call" | custom-call | flops 3221225472 | bytes 14680064 | tf_op jit(solution)/shard_map/pallas_call | solution.py:493
  (1 shorter events, 0.0 us)
Async XLA Ops:
  1.5 2.2 %copy-start.1 = (f32[64,128,128]{2,1,0:T(8,128)S(1)}, f32[64,128,128]{2,1,0:T(8,128)}, u32[]{:S(2)}) copy-start(f32[64,128,128]{2,1,0:T(8,128)} %amplitude_ref.1) | copy-start | bytes 12582916
  3.7 1.2 %copy-start.2 = (bf16[8,256,256]{2,1,0:T(8,128)(2,1)S(1)}, bf16[8,256,256]{2,1,0:T(8,128)(2,1)}, u32[]{:S(2)}) copy-start(bf16[8,256,256]{2,1,0:T(8,128)(2,1)} %constant.8.clone.tables_ref) | copy-start | bytes 3145732
  4.9 0.7 copy-start.3
  5.6 0.7 copy-start.4
  96.2 2.8 %copy-start = (bf16[3,4,2,64,16,128]{5,4,3,2,1,0:T(8,128)(2,1)S(1)}, bf16[3,4,2,64,16,128]{5,4,3,2,1,0:T(8,128)(2,1)}, u32[]{:S(2)}) copy-start(bf16[3,4,2,64,16,128]{5,4,3,2,1,0:T(8,128)(2,1)} %get-tuple-element.10.parts_ref) | copy-start | bytes 18874372
where the time goes:
time: 108 us; the launch traced here: 107 us
  Pallas kernels  98.2 us (91%)
  local copies, waits for them, and re-layouts  7.91 us (7%)
    pallas_call x1, Pallas kernels, waves_to_gradients(): pl.pallas_call(functools.partial(wave_kernel, shares, scan_size), out_sha...  89.7 us
    pallas_call x1, Pallas kernels, backward(): pl.pallas_call(functools.partial(backward_kernel, block_rows), grid=(stri...  8.49 us
    unnamed x10, local copies, waits for them, and re-layouts  7.56 us

commit v1 on v0

--- a/solution.py
+++ b/solution.py
@@ -26,11 +26,11 @@
     return total + jnp.dot(left_high, right_high, preferred_element_type=F32)
 
 
-def wave_kernel(shares, scan_size, spots_ref, freq_ref, amp_ref, live_ref, tables_ref, strip_ref,
-                amplitude_ref, parts_ref, matrix_ref, offset_ref,
-                spots, strips, wide, kept, core_out, core_in, link_out, link_in, zed_out, zed_in,
+def wave_kernel(shares, scan_size, spots_ref, live_ref, freq_hbm, amp_hbm, tables_hbm, strip_ref,
+                amplitude_ref, parts_ref, turned_ref, offset_ref,
+                matrix_ref, freq_ref, amp_ref, tables_ref, spots, strips, wide, kept, core_out, core_in, link_out, link_in, zed_out, zed_in,
                 scan_out, scan_in, near, far, measured, waves, backs, own_far,
-                load_sem, amp_sem, spot_send, spot_recv, pair_send, pair_recv, link_send, link_recv,
+                load_sem, side_sem, spot_send, spot_recv, pair_send, pair_recv, link_send, link_recv,
                 zed_send, zed_recv, scan_send, scan_recv,
                 hop_send, hop_recv, step_send, step_recv, join_send, join_recv):
     chunks, pairs, _, block_rows, group, window = kept.shape
@@ -63,12 +63,23 @@
     def spot_copy(d):
         return remote(spots_ref, spots.at[d - 1], spot_send.at[d - 1], spot_recv.at[d - 1], after[d - 1])
 
+    side_loads = [
+        pltpu.make_async_copy(source, target, side_sem.at[i])
+        for i, (source, target) in enumerate(
+            [
+                (freq_hbm, freq_ref),
+                (amp_hbm, amp_ref),
+                (tables_hbm, tables_ref),
+                (amplitude_ref.at[pl.ds(me * share_rows, share_rows)], measured),
+            ]
+        )
+    ]
+    side_loads[0].start()
+    side_loads[1].start()
     load(0).start()
     load(1).start()
-    load_amplitude = pltpu.make_async_copy(
-        amplitude_ref.at[pl.ds(me * share_rows, share_rows)], measured, amp_sem
-    )
-    load_amplitude.start()
+    side_loads[2].start()
+    side_loads[3].start()
     barrier = pltpu.get_barrier_semaphore()
     peers = [core_mate, link_mate] + before + after
     for peer in peers:
@@ -111,6 +122,8 @@
                         [-im, re], axis=0
                     ).astype(BF16)
 
+    side_loads[0].wait()
+    side_loads[1].wait()
     coefficients(0)
     for d in (1, 2):
         spot_copy(d).wait()
@@ -349,13 +362,16 @@
         after_zed(0, chunk)
     for chunk in range(chunks):
         after_core(1, chunk)
+    for at in range(0, matrix_ref.shape[0], window):
+        turned_ref[:, at : at + window] = matrix_ref[at : at + window, :].astype(F32).T.astype(BF16)
     for chunk in range(chunks):
         after_link(0, chunk)
     for chunk in early:
         after_zed(1, chunk)
     for chunk in range(chunks):
         finish(0, chunk)
-    load_amplitude.wait()
+    side_loads[2].wait()
+    side_loads[3].wait()
     transform(0)
     for chunk in range(chunks):
         after_link(1, chunk)
@@ -400,18 +416,25 @@
     assert field_rows & (field_rows - 1) == 0 and window & (window - 1) == 0
     tail = (block_rows, depth, window)
     vmem = pl.BlockSpec(memory_space=pltpu.VMEM)
-    anywhere = pl.BlockSpec(memory_space=pl.ANY)
+    hbm = pl.BlockSpec(memory_space=pltpu.HBM)
     dma = pltpu.SemaphoreType.DMA
+    stays = [
+        pltpu.with_memory_space_constraint(v, pltpu.HBM) for v in (freq, amp, tables, strip, amplitude)
+    ]
     return pl.pallas_call(
         functools.partial(wave_kernel, shares, scan_size),
         out_shape=[
             jax.ShapeDtypeStruct((3, shares, groups, strip_rows, depth, window), BF16),
-            jax.ShapeDtypeStruct((3 * shares * group, 2 * beams), BF16),
+            jax.ShapeDtypeStruct((2 * beams, 3 * shares * group), BF16),
             jax.ShapeDtypeStruct((2, shares * group, window), jnp.int32),
         ],
-        in_specs=[vmem] * 5 + [anywhere] * 2,
+        in_specs=[vmem] * 2 + [hbm] * 5,
         out_specs=[vmem] * 3,
         scratch_shapes=[
+            pltpu.VMEM((3 * shares * group, 2 * beams), BF16),
+            pltpu.VMEM(freq.shape, jnp.int32),
+            pltpu.VMEM(amp.shape, F32),
+            pltpu.VMEM(tables.shape, BF16),
             pltpu.VMEM((2, 2, per_tile, window), jnp.int32),
             pltpu.VMEM((2, 2, beams, block_rows, window), BF16),
             pltpu.VMEM((2 * beams * block_rows, window), F32),
@@ -431,7 +454,7 @@
             pltpu.VMEM((2, window * share_rows // groups, window), F32),
             pltpu.VMEM((groups, strip_rows, depth, window), BF16),
             dma((2,)),
-            dma,
+            dma((4,)),
             dma((2,)),
             dma((2,)),
             dma((chunks,)),
@@ -450,14 +473,14 @@
             dma((groups, 6, 2)),
         ],
         compiler_params=pltpu.CompilerParams(
-            collective_id=0, has_side_effects=True, vmem_limit_bytes=48 << 20
+            collective_id=0, has_side_effects=True, vmem_limit_bytes=40 << 20
         ),
         cost_estimate=pl.CostEstimate(
             flops=12 * per_tile * beams * strip_rows * window,
             bytes_accessed=4 * beams * strip_rows * window,
             transcendentals=0,
         ),
-    )(spots, freq, amp, live, tables, strip, amplitude)
+    )(spots, live, *stays)
 
 
 def backward_kernel(block_rows, offset_ref, matrix_ref, parts_ref, out_ref, wide):
@@ -547,7 +570,7 @@
     parts, matrix, offsets = waves_to_gradients(
         spots, beam_freq, beam_amp, live, transform_tables(window), smatrix, amplitude, shares, scan_size
     )
-    return backward(matrix.T, offsets, parts, beam_dev)
+    return backward(matrix, offsets, parts, beam_dev)
 
 
 def solution(mesh):

time: 108 us -> 97.2 us (0.900)
  local copies, waits for them, and re-layouts: 7.91 us -> 0.14 us
  Pallas kernels: 98.2 us -> 95.6 us
    unnamed x10 -> x0, local copies, waits for them, and re-layouts: 7.56 us -> none
    pallas_call x1, Pallas kernels: 89.7 us -> 87 us  [waves_to_gradients(): pl.pallas_call(functools.partial(wave_kernel, shares, scan_size), out_sha...]
where the time goes in v1:
time: 97.2 us; the launch traced here: 97.1 us
  Pallas kernels  95.6 us (98%)
    pallas_call x1, Pallas kernels, waves_to_gradients(): pl.pallas_call(functools.partial(wave_kernel, shares, scan_size), out_sha...  87 us
    pallas_call x1, Pallas kernels, backward(): pl.pallas_call(functools.partial(backward_kernel, block_rows), grid=(stri...  8.54 us

profile of v1, /device:TPU:5, one launch (start us, length us, event | category | flops | bytes accessed | tf_op | source)
XLA Modules:
  0.0 97.1 jit_solution(9325087371516290431)
XLA Ops:
  0.7 0.7 pad_add_fusion
  1.3 0.1 broadcast_in_dim.5.live_ref
  1.4 0.1 broadcast_in_dim.4.spots_ref
  1.5 87.0 %shard_map.82 = (bf16[3,4,2,64,16,128]{5,4,3,2,1,0:T(8,128)(2,1)S(1)}, bf16[512,384]{1,0:T(8,128)(2,1)S(1)}, s32[2,128,128]{2,1,0:T(8,128)S(1)}) custom-call(s32[2,64,128]{2,1,0:T(8,128)S(1)} %broadcast_in_dim.4.spots_ref, f32[16,128]{1,0:T(8,128)S(1)} %broadcast_in_dim.5.live_ref, s32[2,256]{1,0:T(2,128)} %freq_hbm.1, f32[2,256]{1,0:T(2,128)} %amp_hbm.1, ...), custom_call_target="tpu_custom_call" | custom-call | flops 1610612736 | bytes 8388608 | tf_op jit(solution)/shard_map/pallas_call | solution.py:424
  88.5 8.5 %shard_map.83 = bf16[2,256,64,128]{3,2,1,0:T(8,128)(2,1)} custom-call(s32[2,128,128]{2,1,0:T(8,128)S(1)} %get-tuple-element.8.offset_ref, bf16[512,384]{1,0:T(8,128)(2,1)S(1)} %get-tuple-element.9.matrix_ref, bf16[3,4,2,64,16,128]{5,4,3,2,1,0:T(8,128)(2,1)S(1)} %get-tuple-element.10.parts_ref), custom_call_target="tpu_custom_call" | custom-call | flops 3221225472 | bytes 14680064 | tf_op jit(solution)/shard_map/pallas_call | solution.py:516
  (1 shorter events, 0.0 us)

commit v2 on v1

--- a/solution.py
+++ b/solution.py
@@ -28,7 +28,7 @@
 
 def wave_kernel(shares, scan_size, spots_ref, live_ref, freq_hbm, amp_hbm, tables_hbm, strip_ref,
                 amplitude_ref, parts_ref, turned_ref, offset_ref,
-                matrix_ref, freq_ref, amp_ref, tables_ref, spots, strips, wide, kept, core_out, core_in, link_out, link_in, zed_out, zed_in,
+                matrix_ref, freq_ref, amp_ref, tables_ref, spots, spread, strips, wide, kept, core_out, core_in, link_out, link_in, zed_out, zed_in,
                 scan_out, scan_in, near, far, measured, waves, backs, own_far,
                 load_sem, side_sem, spot_send, spot_recv, pair_send, pair_recv, link_send, link_recv,
                 zed_send, zed_recv, scan_send, scan_recv,
@@ -90,11 +90,14 @@
 
     def coefficients(d):
         source = spots_ref if d == 0 else spots.at[d - 1]
+        for c in range(2):
+            line = jnp.broadcast_to(source[c : c + 1, :].astype(F32), (window, window))
+            spread[c] = line.T.astype(jnp.int32)
         tile_id = lax.rem(tile + scan_size - d, scan_size)
         for s in range(shares):
             here = pl.ds(share_ids[s] * share_rows, share_rows)
-            rows = source[0, here, :]
-            cols = source[1, here, :]
+            rows = spread[0, here, :]
+            cols = spread[1, here, :]
             base = (d * shares + s) * group
             if d != 1:
                 at = s * group
@@ -357,23 +360,28 @@
         compute(chunk)
         if chunk:
             after_core(0, chunk - 1)
+            if chunk - 1 in early:
+                after_core(1, chunk - 1)
     after_core(0, chunks - 1)
     for chunk in early:
         after_zed(0, chunk)
-    for chunk in range(chunks):
+    for chunk in range(chunks // 2, chunks):
         after_core(1, chunk)
     for at in range(0, matrix_ref.shape[0], window):
         turned_ref[:, at : at + window] = matrix_ref[at : at + window, :].astype(F32).T.astype(BF16)
-    for chunk in range(chunks):
+    for chunk in early:
+        after_link(0, chunk)
+        after_zed(1, chunk)
+    for chunk in range(chunks // 2, chunks):
         after_link(0, chunk)
     for chunk in early:
-        after_zed(1, chunk)
+        after_link(1, chunk)
     for chunk in range(chunks):
         finish(0, chunk)
     side_loads[2].wait()
     side_loads[3].wait()
     transform(0)
-    for chunk in range(chunks):
+    for chunk in range(chunks // 2, chunks):
         after_link(1, chunk)
     for chunk in range(chunks):
         finish(1, chunk)
@@ -402,10 +410,9 @@
             over_scan(d, s, g, h).wait_send()
 
 
-def waves_to_gradients(spots, freq, amp, live, tables, strip, amplitude, shares, scan_size,
+def waves_to_gradients(per_tile, spots, freq, amp, live, tables, strip, amplitude, shares, scan_size,
                        groups=2, block_rows=8):
     _, beams, strip_rows, window = strip.shape
-    per_tile = spots.shape[1]
     share_rows = per_tile // shares
     group = 2 * share_rows
     depth = group // groups
@@ -435,7 +442,8 @@
             pltpu.VMEM(freq.shape, jnp.int32),
             pltpu.VMEM(amp.shape, F32),
             pltpu.VMEM(tables.shape, BF16),
-            pltpu.VMEM((2, 2, per_tile, window), jnp.int32),
+            pltpu.VMEM((2,) + spots.shape, jnp.int32),
+            pltpu.VMEM((2, window, window), jnp.int32),
             pltpu.VMEM((2, 2, beams, block_rows, window), BF16),
             pltpu.VMEM((2 * beams * block_rows, window), F32),
             pltpu.VMEM((chunks, pairs, 3, block_rows, group, window), F32),
@@ -561,14 +569,13 @@
     shares = lax.axis_size("beam")
     share_rows = per_tile // shares
     assert window == 2 * smatrix.shape[2]
-    spots = jnp.broadcast_to(
-        jnp.stack([row_offset, col_offset])[:, :, None], (2, per_tile, window)
-    )
+    assert per_tile <= window
+    spots = jnp.pad(jnp.stack([row_offset, col_offset]), ((0, 6), (0, window - per_tile)))
     first_row = lax.axis_index("beam") * share_rows
     live = (first_row + jnp.arange(share_rows, dtype=jnp.int32) < counts[0]).astype(F32)
     live = jnp.broadcast_to(live[:, None], (share_rows, window))
     parts, matrix, offsets = waves_to_gradients(
-        spots, beam_freq, beam_amp, live, transform_tables(window), smatrix, amplitude, shares, scan_size
+        per_tile, spots, beam_freq, beam_amp, live, transform_tables(window), smatrix, amplitude, shares, scan_size
     )
     return backward(matrix, offsets, parts, beam_dev)
 

time: 97.2 us -> 93 us (0.957)
  Pallas kernels: 95.6 us -> 90.8 us
    pallas_call x1, Pallas kernels: 87 us -> 82.3 us  [waves_to_gradients(): pl.pallas_call(functools.partial(wave_kernel, shares, scan_size), out_sha...]
where the time goes in v2:
time: 93 us; the launch traced here: 92.2 us
  Pallas kernels  90.8 us (98%)
    pallas_call x1, Pallas kernels, waves_to_gradients(): pl.pallas_call(functools.partial(wave_kernel, shares, scan_size), out_sha...  82.3 us
    pallas_call x1, Pallas kernels, backward(): pl.pallas_call(functools.partial(backward_kernel, block_rows), grid=(stri...  8.55 us

profile of v2, /device:TPU:5, one launch (start us, length us, event | category | flops | bytes accessed | tf_op | source)
XLA Modules:
  0.0 92.2 jit_solution(3118435749656874658)
XLA Ops:
  0.7 0.7 pad_add_fusion
  1.4 0.1 broadcast_in_dim.2.live_ref
  1.4 82.3 %shard_map.82 = (bf16[3,4,2,64,16,128]{5,4,3,2,1,0:T(8,128)(2,1)S(1)}, bf16[512,384]{1,0:T(8,128)(2,1)S(1)}, s32[2,128,128]{2,1,0:T(8,128)S(1)}) custom-call(s32[8,128]{1,0:T(8,128)S(1)} %pad.4.spots_ref, f32[16,128]{1,0:T(8,128)S(1)} %broadcast_in_dim.2.live_ref, s32[2,256]{1,0:T(2,128)} %freq_hbm.1, f32[2,256]{1,0:T(2,128)} %amp_hbm.1, ...), custom_call_target="tpu_custom_call" | custom-call | flops 1610612736 | bytes 8388608 | tf_op jit(solution)/shard_map/pallas_call | solution.py:431
  83.7 8.5 %shard_map.83 = bf16[2,256,64,128]{3,2,1,0:T(8,128)(2,1)} custom-call(s32[2,128,128]{2,1,0:T(8,128)S(1)} %get-tuple-element.8.offset_ref, bf16[512,384]{1,0:T(8,128)(2,1)S(1)} %get-tuple-element.9.matrix_ref, bf16[3,4,2,64,16,128]{5,4,3,2,1,0:T(8,128)(2,1)S(1)} %get-tuple-element.10.parts_ref), custom_call_target="tpu_custom_call" | custom-call | flops 3221225472 | bytes 14680064 | tf_op jit(solution)/shard_map/pallas_call | solution.py:524
  (2 shorter events, 0.0 us)

commit v3 on v2

--- a/solution.py
+++ b/solution.py
@@ -32,13 +32,15 @@
                 scan_out, scan_in, near, far, measured, waves, backs, own_far,
                 load_sem, side_sem, spot_send, spot_recv, pair_send, pair_recv, link_send, link_recv,
                 zed_send, zed_recv, scan_send, scan_recv,
-                hop_send, hop_recv, step_send, step_recv, join_send, join_recv):
+                hop_send, hop_recv, step_send, step_recv, join_send, join_recv,
+                relay_in, hop_in, relay_send, relay_recv, pass_send, far_send, far_recv, last_send):
     chunks, pairs, _, block_rows, group, window = kept.shape
     _, _, groups, strip_rows, depth, _ = parts_ref.shape
     beams = strip_ref.shape[1]
     share = depth // 2
     share_rows = group // 2
     field_rows = strip_rows * scan_size
+    cut = zed_out.shape[1]
     me = lax.axis_index("beam")
     tile = lax.axis_index("scan")
     core_id = me + 1 - 2 * lax.rem(me, 2)
@@ -138,7 +140,7 @@
         )
 
     def to_link(g, chunk, late):
-        if chunk >= chunks // 2:
+        if chunk >= cut:
             pieces = slice(0, 3)
         elif late:
             pieces = slice(0, 1)
@@ -161,6 +163,29 @@
             scan_out.at[g, chunk, which], scan_in.at[g, chunk, which],
             scan_send.at[g, chunk, which], scan_recv.at[g, chunk, which], before[which],
         )
+
+    odd = lax.rem(tile, 2) == 1
+    even = lax.rem(tile, 2) == 0
+
+    def to_relay(g, chunk):
+        at = chunk // 2
+        return remote(
+            scan_out.at[g, chunk, 0], relay_in.at[g, at],
+            relay_send.at[g, at], relay_recv.at[g, at], after[0],
+        )
+
+    def from_relay(g, chunk):
+        at = chunk // 2
+        return remote(
+            relay_in.at[g, at], scan_in.at[g, chunk, 0],
+            pass_send.at[g, at], scan_recv.at[g, chunk, 0], before[1],
+        )
+
+    def pass_on(g, chunk):
+        @pl.when(odd)
+        def _():
+            to_relay(g, chunk).wait_recv()
+            from_relay(g, chunk).start()
 
     def compute(chunk):
         load(chunk).wait()
@@ -201,7 +226,7 @@
         if g == 0:
             to_core(chunk).wait_recv()
         link_out[g, chunk, 1] = held(g, chunk, 1, 1).astype(BF16)
-        if chunk < chunks // 2:
+        if chunk < cut:
             for s in range(2):
                 zed_out[g, chunk, s] = held(g, chunk, s, 2).astype(BF16)
             to_zed(g, chunk).start()
@@ -220,16 +245,20 @@
 
     def after_link(g, chunk):
         to_link(g, chunk, 0).wait_recv()
-        for d in (1, 2) if chunk >= chunks // 2 else (1,):
+        for d in (1, 2) if chunk >= cut else (1,):
             scan_out[g, chunk, d - 1] = (
                 held(g, chunk, 0, d) + link_in[g, chunk, d].astype(F32)
             ).astype(BF16)
-            to_scan(g, chunk, d - 1).start()
-        if chunk >= chunks // 2:
+            if d == 1 and chunk % 2:
+                pl.when(odd)(to_scan(g, chunk, 0).start)
+                pl.when(even)(to_relay(g, chunk).start)
+            else:
+                to_scan(g, chunk, d - 1).start()
+        if chunk >= cut:
             near[g, rows_of(chunk)] = held(g, chunk, 0, 0) + link_in[g, chunk, 0].astype(F32)
 
     def finish(g, chunk):
-        if chunk < chunks // 2:
+        if chunk < cut:
             to_link(g, chunk, 1).wait_recv()
             near[g, rows_of(chunk)] = (
                 held(g, chunk, 0, 0)
@@ -238,12 +267,12 @@
             )
         to_scan(g, chunk, 0).wait_recv()
         far[g, rows_of(chunk)] = scan_in[g, chunk, 0].astype(F32)
-        if chunk >= chunks // 2:
+        if chunk >= cut:
             to_scan(g, chunk, 1).wait_recv()
             near[g, rows_of(chunk)] += scan_in[g, chunk, 1].astype(F32)
 
-    half_rows = strip_rows // 2
-    halves = [pl.ds(h * half_rows, half_rows) for h in range(2)]
+    low_rows = strip_rows // 4
+    halves = [pl.ds(0, low_rows), pl.ds(low_rows, strip_rows - low_rows)]
     hop_at = {(0, 0): 0, (0, 1): 1, (1, 0): 2, (1, 1): 3, (2, 0): 4}
     step_at = {(1, 0, 0): 0, (1, 0, 1): 1, (2, 0, 0): 2, (2, 0, 1): 3, (2, 1, 1): 4}
 
@@ -267,6 +296,18 @@
         return remote(
             source.at[halves[h]], parts_ref.at[d, s, g, halves[h]],
             step_send.at[g, at], step_recv.at[g, at], after[d - 1],
+        )
+
+    def far_relay(h):
+        return remote(
+            own_far.at[0, halves[h]], hop_in.at[halves[h]],
+            far_send.at[h], far_recv.at[h], before[0],
+        )
+
+    def far_pass(h):
+        return remote(
+            hop_in.at[halves[h]], parts_ref.at[1, 0, 0, halves[h]],
+            last_send.at[h], step_recv.at[0, step_at[1, 0, h]], after[1],
         )
 
     def by_columns(high, low, table):
@@ -322,7 +363,11 @@
             if half:
                 own_far[g] = value
                 for h in range(2):
-                    over_scan(1, 0, g, h).start()
+                    if g == 0:
+                        pl.when(even)(over_scan(1, 0, g, h).start)
+                        pl.when(odd)(far_relay(h).start)
+                    else:
+                        over_scan(1, 0, g, h).start()
             else:
                 parts_ref[0, 0, g] = value
                 for h in (1, 0):
@@ -342,6 +387,12 @@
         if scan:
             over_scan(2, 1, g, h).start()
         over_core(d, 1, g, h).start()
+
+    def pass_far(h):
+        @pl.when(even)
+        def _():
+            far_relay(h).wait_recv()
+            far_pass(h).start()
 
     def relay(g):
         got_scan(1, 0, g, 0, True)
@@ -355,7 +406,7 @@
         got_scan(2, 1, g, 1, False)
         got_link(2, g, 0, False)
 
-    early = range(chunks // 2)
+    early = range(cut)
     for chunk in range(chunks):
         compute(chunk)
         if chunk:
@@ -365,15 +416,17 @@
     after_core(0, chunks - 1)
     for chunk in early:
         after_zed(0, chunk)
-    for chunk in range(chunks // 2, chunks):
+    for chunk in range(cut, chunks):
         after_core(1, chunk)
     for at in range(0, matrix_ref.shape[0], window):
         turned_ref[:, at : at + window] = matrix_ref[at : at + window, :].astype(F32).T.astype(BF16)
     for chunk in early:
         after_link(0, chunk)
         after_zed(1, chunk)
-    for chunk in range(chunks // 2, chunks):
+    for chunk in range(cut, chunks):
         after_link(0, chunk)
+    for chunk in range(1, chunks, 2):
+        pass_on(0, chunk)
     for chunk in early:
         after_link(1, chunk)
     for chunk in range(chunks):
@@ -381,8 +434,12 @@
     side_loads[2].wait()
     side_loads[3].wait()
     transform(0)
-    for chunk in range(chunks // 2, chunks):
+    for chunk in range(cut, chunks):
         after_link(1, chunk)
+    for chunk in range(1, chunks, 2):
+        pass_on(1, chunk)
+    for h in range(2):
+        pass_far(h)
     for chunk in range(chunks):
         finish(1, chunk)
     transform(1)
@@ -393,8 +450,13 @@
         to_core(chunk).wait_send()
         for g in range(groups):
             to_link(g, chunk, 0).wait_send()
-            to_scan(g, chunk, 0).wait_send()
-            if chunk < chunks // 2:
+            if chunk % 2:
+                pl.when(odd)(to_scan(g, chunk, 0).wait_send)
+                pl.when(even)(to_relay(g, chunk).wait_send)
+                pl.when(odd)(from_relay(g, chunk).wait_send)
+            else:
+                to_scan(g, chunk, 0).wait_send()
+            if chunk < cut:
                 to_link(g, chunk, 1).wait_send()
                 to_zed(g, chunk).wait_send()
             else:
@@ -407,7 +469,12 @@
         for d, h in hop_at:
             over_link(d, g, h).wait_send()
         for d, s, h in step_at:
-            over_scan(d, s, g, h).wait_send()
+            if d == 1 and g == 0:
+                pl.when(even)(over_scan(d, s, g, h).wait_send)
+                pl.when(odd)(far_relay(h).wait_send)
+                pl.when(even)(far_pass(h).wait_send)
+            else:
+                over_scan(d, s, g, h).wait_send()
 
 
 def waves_to_gradients(per_tile, spots, freq, amp, live, tables, strip, amplitude, shares, scan_size,
@@ -418,8 +485,9 @@
     depth = group // groups
     field_rows = strip_rows * scan_size
     chunks = strip_rows // block_rows
+    cut = chunks // 2
     pairs = shares // 2
-    assert groups == 2 and shares == 4 and scan_size > 4 and chunks % 2 == 0
+    assert groups == 2 and shares == 4 and scan_size > 4 and scan_size % 2 == 0 and chunks % 4 == 0
     assert field_rows & (field_rows - 1) == 0 and window & (window - 1) == 0
     tail = (block_rows, depth, window)
     vmem = pl.BlockSpec(memory_space=pltpu.VMEM)
@@ -451,8 +519,8 @@
             pltpu.VMEM((chunks, pairs, 3, block_rows, group, window), BF16),
             pltpu.VMEM((groups, chunks, 3) + tail, BF16),
             pltpu.VMEM((groups, chunks, 3) + tail, BF16),
-            pltpu.VMEM((groups, chunks // 2, 2) + tail, BF16),
-            pltpu.VMEM((groups, chunks // 2, 2) + tail, BF16),
+            pltpu.VMEM((groups, cut, 2) + tail, BF16),
+            pltpu.VMEM((groups, cut, 2) + tail, BF16),
             pltpu.VMEM((groups, chunks, 2) + tail, BF16),
             pltpu.VMEM((groups, chunks, 2) + tail, BF16),
             pltpu.VMEM((groups, strip_rows, depth, window), F32),
@@ -469,8 +537,8 @@
             dma((chunks,)),
             dma((groups, chunks, 2)),
             dma((groups, chunks, 2)),
-            dma((groups, chunks // 2)),
-            dma((groups, chunks // 2)),
+            dma((groups, cut)),
+            dma((groups, cut)),
             dma((groups, chunks, 2)),
             dma((groups, chunks, 2)),
             dma((groups, 5)),
@@ -479,6 +547,14 @@
             dma((groups, 5)),
             dma((groups, 6, 2)),
             dma((groups, 6, 2)),
+            pltpu.VMEM((groups, chunks // 2) + tail, BF16),
+            pltpu.VMEM((strip_rows, depth, window), BF16),
+            dma((groups, chunks // 2)),
+            dma((groups, chunks // 2)),
+            dma((groups, chunks // 2)),
+            dma((2,)),
+            dma((2,)),
+            dma((2,)),
         ],
         compiler_params=pltpu.CompilerParams(
             collective_id=0, has_side_effects=True, vmem_limit_bytes=40 << 20

time: 93 us -> 90 us (0.968)
  Pallas kernels: 90.8 us -> 87.3 us
    pallas_call x1, Pallas kernels: 82.3 us -> 78.7 us  [waves_to_gradients(): pl.pallas_call(functools.partial(wave_kernel, shares, scan_size), out_sha...]
where the time goes in v3:
time: 90 us; the launch traced here: 88.7 us
  Pallas kernels  87.3 us (97%)
    pallas_call x1, Pallas kernels, waves_to_gradients(): pl.pallas_call(functools.partial(wave_kernel, shares, scan_size), out_sha...  78.7 us
    pallas_call x1, Pallas kernels, backward(): pl.pallas_call(functools.partial(backward_kernel, block_rows), grid=(stri...  8.54 us

profile of v3, /device:TPU:5, one launch (start us, length us, event | category | flops | bytes accessed | tf_op | source)
XLA Modules:
  0.0 88.7 jit_solution(3154533642760681516)
XLA Ops:
  0.7 0.7 pad_add_fusion
  1.4 0.1 broadcast_in_dim.2.live_ref
  1.4 78.7 %shard_map.82 = (bf16[3,4,2,64,16,128]{5,4,3,2,1,0:T(8,128)(2,1)S(1)}, bf16[512,384]{1,0:T(8,128)(2,1)S(1)}, s32[2,128,128]{2,1,0:T(8,128)S(1)}) custom-call(s32[8,128]{1,0:T(8,128)S(1)} %pad.4.spots_ref, f32[16,128]{1,0:T(8,128)S(1)} %broadcast_in_dim.2.live_ref, s32[2,256]{1,0:T(2,128)} %freq_hbm.1, f32[2,256]{1,0:T(2,128)} %amp_hbm.1, ...), custom_call_target="tpu_custom_call" | custom-call | flops 1610612736 | bytes 8388608 | tf_op jit(solution)/shard_map/pallas_call | solution.py:499
  80.2 8.5 %shard_map.83 = bf16[2,256,64,128]{3,2,1,0:T(8,128)(2,1)} custom-call(s32[2,128,128]{2,1,0:T(8,128)S(1)} %get-tuple-element.8.offset_ref, bf16[512,384]{1,0:T(8,128)(2,1)S(1)} %get-tuple-element.9.matrix_ref, bf16[3,4,2,64,16,128]{5,4,3,2,1,0:T(8,128)(2,1)S(1)} %get-tuple-element.10.parts_ref), custom_call_target="tpu_custom_call" | custom-call | flops 3221225472 | bytes 14680064 | tf_op jit(solution)/shard_map/pallas_call | solution.py:600
  (2 shorter events, 0.0 us)
